TPU v7x, 512 devices: a whole 4x8x8 slice. The times are simulated.
512 devices in a mesh: sec: 2 (over y_lo), exp: 32 (over y_hi, x, core), hid: 8 (over z).
Axes of the slice: x: 4, y: 8 (y_hi: 4, y_lo: 2; y = y_hi * 2 + y_lo), z: 8, core: 2. Of those that a mesh axis runs over, the one named last changes fastest.
Arguments:
- tokens: bfloat16 [1024, 4096], P('exp', ('sec', 'hid')), may hold values from -1200 to 1200
- norm_gain: bfloat16 [4096], P(('sec', 'hid')), may hold values from 0.5 to 2
- route_weight: float32 [1024, 2], P('exp'), may hold values from 0.1 to 1
- block_experts: int32 [8, 2], replicated, may hold values from 0 to 7, all different within a row; in each aligned block of 8 rows (0 to 7, 8 to 15, ...) at most 4 rows name the same one
- w_gate: bfloat16 [2, 4096, 32768], P('sec', None, ('exp', 'hid')), may hold values from -0.09375 to 0.09375
- w_up: bfloat16 [2, 4096, 32768], P('sec', None, ('exp', 'hid')), may hold values from -0.09375 to 0.09375
- w_down: bfloat16 [2, 32768, 4096], P('sec', ('exp', 'hid')), may hold values from -0.0625 to 0.0625
Outputs:
- moe_out: bfloat16 [1024, 4096], P('exp', ('sec', 'hid'))
Inputs may be any that keep to these rules, and one draw needn't show every extreme that they name: `block_experts`: each row names 2 different experts; no expert is named by more than 4 rows, a bound that some block reaches; every expert is named by some row.
All inputs are finite; a program needn't handle non-finite values.
Results may differ from a plain program's by a relative error of at most 0.018.
Values may be sent and summed in bfloat16 or wider, within the bound.
No kernel may reach another device: no remote copies, remote signals or barrier semaphores. Data moves between devices by JAX's collectives and lax.ppermute only.
A program may use at most 64 MiB of HBM per device.

v0:
```python
import jax
import jax.numpy as jnp
from jax import lax
from jax.sharding import PartitionSpec as P

D = 4096
EXPERTS = 8
BLK = 128
MOST = 4


def per_device(tokens, norm_gain, route_weight, block_experts, w_gate, w_up, w_down):
    exp_devices = lax.axis_size("exp")
    group_size = exp_devices // EXPERTS
    my_expert = lax.axis_index("exp") // group_size
    tok_local = tokens.shape[0]
    total_rows = tok_local * exp_devices
    num_blocks = total_rows // BLK
    slot_count = MOST
    gate_local = w_gate[0]
    up_local = w_up[0]
    down_local = w_down[0]
    block_hit = jnp.any(block_experts == my_expert, axis=1)
    hit_flags = block_hit.astype(jnp.int32)
    slot_of_block = jnp.where(block_hit, jnp.cumsum(hit_flags) - 1, -1)
    slot_ids = jnp.arange(slot_count, dtype=jnp.int32)
    slot_match = slot_of_block[None, :] == slot_ids[:, None]
    block_ids = jnp.arange(num_blocks, dtype=jnp.int32)
    block_of_slot = jnp.sum(jnp.where(slot_match, block_ids[None, :], 0), axis=1)
    slot_valid = jnp.any(slot_match, axis=1)
    values = tokens.astype(jnp.float32)
    square_part = jnp.sum(values * values, axis=1)
    square_total = lax.psum(square_part, ("sec", "hid"))
    rms_value = jnp.sqrt(square_total / D + 1e-05)
    normed = (values * norm_gain.astype(jnp.float32) / rms_value[:, None]).astype(jnp.bfloat16)
    gathered = lax.all_gather(normed, "exp", axis=0, tiled=True)
    width = gathered.shape[1]
    picked = jnp.take(gathered.reshape(num_blocks, BLK, width), block_of_slot, axis=0)
    picked = jnp.where(slot_valid[:, None, None], picked, jnp.zeros_like(picked))
    picked_rows = picked.reshape(slot_count * BLK, width)
    feature_piece = lax.all_gather(picked_rows, ("sec", "hid"), axis=1, tiled=True)
    gate_acc = jnp.dot(feature_piece, gate_local, preferred_element_type=jnp.float32)
    up_acc = jnp.dot(feature_piece, up_local, preferred_element_type=jnp.float32)
    activated = (jax.nn.silu(gate_acc) * up_acc).astype(jnp.bfloat16)
    contribution = jnp.dot(activated, down_local, preferred_element_type=jnp.float32)
    term_vals = contribution.astype(jnp.bfloat16)
    own_rows = lax.axis_index("exp") * tok_local + jnp.arange(tok_local, dtype=jnp.int32)
    own_blocks = own_rows // BLK
    own_experts = jnp.take(block_experts, own_blocks, axis=0)
    source_expert = jnp.arange(exp_devices, dtype=jnp.int32) // group_size
    factor = jnp.sum(
        jnp.where(
            own_experts[None, :, :] == source_expert[:, None, None], route_weight[None, :, :], 0.0
        ),
        axis=2,
    )
    reduced = lax.psum_scatter(term_vals, ("sec", "hid"), scatter_dimension=1, tiled=True).astype(
        jnp.float32
    )
    width = reduced.shape[1]
    slot_grid = reduced.reshape(slot_count, BLK, width)
    safe_slot = jnp.maximum(slot_of_block, 0)
    expanded = jnp.take(slot_grid, safe_slot, axis=0)
    expanded = jnp.where(block_hit[:, None, None], expanded, jnp.zeros_like(expanded))
    outgoing = expanded.reshape(exp_devices, tok_local, width)
    received = lax.all_to_all(
        outgoing.astype(jnp.bfloat16), "exp", split_axis=0, concat_axis=0, tiled=True
    ).astype(outgoing.dtype)
    result = jnp.sum(received * factor[:, :, None], axis=0)
    return result.astype(jnp.bfloat16)


def solution(mesh):
    return jax.shard_map(
        per_device,
        mesh=mesh,
        in_specs=(
            P("exp", ("sec", "hid")),
            P(("sec", "hid")),
            P("exp", None),
            P(),
            P("sec", None, ("exp", "hid")),
            P("sec", None, ("exp", "hid")),
            P("sec", ("exp", "hid"), None),
        ),
        out_specs=P("exp", ("sec", "hid")),
        check_vma=False,
    )
```

profile of v0, /device:TPU:9, one launch (start us, length us, event | category | flops | bytes accessed | tf_op | source)
XLA Modules:
  0.0 313.3 jit_solution(5382523622550973638)
XLA Ops:
  6.5 0.8 compare_reduce_fusion
  7.4 0.2 reduce-window.4
  7.6 0.1 select_reduce_fusion.1
  7.7 0.1 fusion.16
  7.9 0.8 fusion.15
  8.7 32.5 %psum.7 = f32[32]{0:T(128)S(1)} all-reduce(f32[32]{0:T(128)S(1)} %fusion.15), channel_id=1, replica_groups=mesh['sec'=2,'exp'=32,'hid'=8] {'sec','hid'}, use_global_device_ids=true, to_apply=%region_5.6 | all-reduce | flops 32 | bytes 256 | tf_op jit(solution)/shard_map/psum | solution.py:33
  41.2 0.7 convert_element_type.37
  41.9 0.8 fusion.14
  42.7 54.8 %all_gather.6 = bf16[1024,256]{1,0:T(8,128)(2,1)S(1)} all-gather(bf16[32,256]{1,0:T(8,128)(2,1)S(1)} %fusion.14), channel_id=1, replica_groups=mesh['sec'=2,'exp'=32,'hid'=8] {'exp'}, dimensions={0}, use_global_device_ids=true | all-gather | bytes 540672 | tf_op jit(solution)/shard_map/all_gather | solution.py:36
  97.4 0.6 gather_fusion
  98.0 0.1 broadcast_bitcast_fusion
  98.1 0.9 fusion.6
  99.0 0.0 all-gather.2.cloned.1.call-update
  99.0 0.0 reduce-scatter.2.cloned.1.call-start
  99.1 70.2 %all-gather.2.cloned.1.call-done = bf16[512,4096]{1,0:T(8,128)(2,1)} async-done(((bf16[512,256]{1,0:T(8,128)(2,1)}), bf16[512,4096]{1,0:T(8,128)(2,1)}) %all-gather.2.cloned.1.call-update) | async-done | bytes 4194320 | tf_op jit(solution)/shard_map/all_gather | solution.py:41
  169.3 3.7 %fusion.4 = f32[512,128]{1,0:T(8,128)S(1)} fusion(bf16[512,4096]{1,0:T(8,128)(2,1)} %all-gather.2.cloned.1.call-done, bf16[1,4096,128]{2,1,0:T(8,128)(2,1)} %param.11), kind=kOutput, calls=%fused_computation.8 | convolution fusion | flops 536870912 | bytes 5505024 | tf_op jit(solution)/shard_map/dot_general | solution.py:42
  173.1 8.6 %convolution_convert_fusion = bf16[512,4096]{1,0:T(8,128)(2,1)} fusion(bf16[512,4096]{1,0:T(8,128)(2,1)} %all-gather.2.cloned.1.call-done, bf16[1,128,4096]{2,1,0:T(8,128)(2,1)S(1)} %copy-done, bf16[1,4096,128]{2,1,0:T(8,128)(2,1)S(1)} %copy-done.1, f32[512,128]{1,0:T(8,128)S(1)} %fusion.4), kind=kOutput, calls=%fused_computation.3 | convolution fusion | flops 1076232192 | bytes 10747904 | tf_op jit(solution)/shard_map/dot_general | solution.py:45
  181.7 0.1 broadcast_in_dim.108
  181.8 0.1 broadcast_in_dim.109
  181.9 0.1 broadcast_in_dim.105
  182.0 0.1 broadcast_in_dim.106
  182.1 80.8 %reduce-scatter.2.cloned.1.call-done = bf16[512,256]{1,0:T(8,128)(2,1)} async-done(((bf16[512,4096]{1,0:T(8,128)(2,1)}), bf16[512,256]{1,0:T(8,128)(2,1)}) %reduce-scatter.2.cloned.1.call-update) | async-done | bytes 262160 | tf_op jit(solution)/shard_map/reduce_scatter | solution.py:57
  262.9 1.5 gather_fusion.1
  264.4 1.0 select_convert_fusion
  265.5 21.9 %all-to-all-start = ((bf16[32,32,256]{2,1,0:T(8,128)(2,1)}), bf16[32,32,256]{2,1,0:T(8,128)(2,1)S(1)}, u32[]{:S(2)}, u32[]{:S(2)}) async-start(bf16[32,32,256]{2,1,0:T(8,128)(2,1)} %select_convert_fusion), calls=%async_computation.1 | async-start | bytes 1048576 | tf_op jit(solution)/shard_map/all_to_all | solution.py:66
  287.4 0.1 copy.12
  287.5 0.6 gather_fusion.2
  288.1 0.1 broadcast_select_fusion
  288.2 0.1 copy.13
  288.3 0.1 select_reduce_fusion
  288.3 17.3 %all-to-all-done = bf16[32,32,256]{2,1,0:T(8,128)(2,1)S(1)} async-done(((bf16[32,32,256]{2,1,0:T(8,128)(2,1)}), bf16[32,32,256]{2,1,0:T(8,128)(2,1)S(1)}, u32[]{:S(2)}, u32[]{:S(2)}) %all-to-all-start) | async-done | bytes 524320 | tf_op jit(solution)/shard_map/all_to_all | solution.py:66
  305.6 0.8 multiply_reduce_fusion
  (22 shorter events, 0.1 us)
Async XLA Ops:
  6.5 166.5 %copy-start = (bf16[1,128,4096]{2,1,0:T(8,128)(2,1)S(1)}, bf16[1,128,4096]{2,1,0:T(8,128)(2,1)}, u32[]{:S(2)}) copy-start(bf16[1,128,4096]{2,1,0:T(8,128)(2,1)} %param.13) | copy-start | bytes 3145732
  6.5 166.5 %copy-start.1 = (bf16[1,4096,128]{2,1,0:T(8,128)(2,1)S(1)}, bf16[1,4096,128]{2,1,0:T(8,128)(2,1)}, u32[]{:S(2)}) copy-start(bf16[1,4096,128]{2,1,0:T(8,128)(2,1)} %param.12) | copy-start | bytes 3145732
  6.5 162.8 %all-gather.2.cloned.1.call-start = ((), (), s32[]{:S(2)}) async-start(), calls=%async_computation.2 | async-start | bytes 4456448 | tf_op jit(solution)/shard_map/all_gather | solution.py:41
  99.0 163.9 %reduce-scatter.2.cloned.1.call-start = ((), (), s32[]{:S(2)}) async-start(), calls=%async_computation.3 | async-start | bytes 4456448 | tf_op jit(solution)/shard_map/reduce_scatter | solution.py:57
  181.7 105.7 %copy-start.2 = (s32[8,2]{0,1:T(2,128)S(1)}, s32[8,2]{0,1:T(2,128)}, u32[]{:S(2)}) copy-start(s32[8,2]{0,1:T(2,128)} %param.10) | copy-start | bytes 196
  181.7 106.6 %copy-start.3 = (f32[32,2]{0,1:T(2,128)S(1)}, f32[32,2]{0,1:T(2,128)}, u32[]{:S(2)}) copy-start(f32[32,2]{0,1:T(2,128)} %param.9) | copy-start | bytes 772
  265.5 40.2 %all-to-all-start = ((bf16[32,32,256]{2,1,0:T(8,128)(2,1)}), bf16[32,32,256]{2,1,0:T(8,128)(2,1)S(1)}, u32[]{:S(2)}, u32[]{:S(2)}) async-start(bf16[32,32,256]{2,1,0:T(8,128)(2,1)} %select_convert_fusion), calls=%async_computation.1 | async-start | bytes 1048576 | tf_op jit(solution)/shard_map/all_to_all | solution.py:66
Sparse Core Ops, SparseCore 0:
  99.1 70.1 all-gather.1
  181.8 81.0 reduce-scatter.1
where the time goes:
time: 314 us; the launch traced here: 313 us
  waiting for transfers between devices  168 us (54%)
  blocking collectives  87.3 us (28%)
  starting transfers between devices  22 us (7%)
  between operations  13.5 us (4%)
  matrix products  12.4 us (4%)
  other arithmetic  6.52 us (2%)
  local copies, waits for them, and re-layouts  3.24 us (1%)
    reduce_scatter x1, waiting for transfers between devices, per_device(): lax.psum_scatter(term_vals, ('sec', 'hid'), scatter_dimension=1, tiled=True)  80.8 us
    all_gather x1, waiting for transfers between devices, per_device(): lax.all_gather(picked_rows, ('sec', 'hid'), axis=1, tiled=True)  70.2 us
    all_gather x1, blocking collectives, per_device(): gathered = lax.all_gather(normed, 'exp', axis=0, tiled=True)  54.8 us
    psum x1, blocking collectives, per_device(): square_total = lax.psum(square_part, ('sec', 'hid'))  32.5 us
    all_to_all x1, starting transfers between devices, per_device(): lax.all_to_all(outgoing.astype(jnp.bfloat16), 'exp', split_axis=0, concat...  21.9 us
    all_to_all x1, waiting for transfers between devices, per_device(): lax.all_to_all(outgoing.astype(jnp.bfloat16), 'exp', split_axis=0, concat...  17.3 us
    dot_general x1, matrix products, per_device(): jnp.dot(activated, down_local, preferred_element_type=jnp.float32)  8.64 us
  transfers between devices with their start and end apart: 3, of which 3 were waited for; matrix products, arithmetic and copies ran while one was open for 0% of the time, Pallas kernels for 0%

commit v1 on v0

--- a/solution.py
+++ b/solution.py
@@ -30,7 +30,8 @@
     slot_valid = jnp.any(slot_match, axis=1)
     values = tokens.astype(jnp.float32)
     square_part = jnp.sum(values * values, axis=1)
-    square_total = lax.psum(square_part, ("sec", "hid"))
+    one_axis = lax.psum(square_part, "sec")
+    square_total = lax.psum(one_axis, "hid")
     rms_value = jnp.sqrt(square_total / D + 1e-05)
     normed = (values * norm_gain.astype(jnp.float32) / rms_value[:, None]).astype(jnp.bfloat16)
     gathered = lax.all_gather(normed, "exp", axis=0, tiled=True)

time: 314 us -> 302 us (0.962)
  blocking collectives: 87.3 us -> 74.5 us
    psum x1 -> x2, blocking collectives: 32.5 us -> 23.3 us  [the longest x1 19.5 us: per_device(): square_total = lax.psum(one_axis, 'hid')]
    all_gather x1, blocking collectives: 54.8 us -> 51.2 us  [per_device(): gathered = lax.all_gather(normed, 'exp', axis=0, tiled=True)]
where the time goes in v1:
time: 302 us; the launch traced here: 301 us
  waiting for transfers between devices  170 us (56%)
  blocking collectives  74.5 us (25%)
  starting transfers between devices  21 us (7%)
  between operations  13.5 us (4%)
  matrix products  12.4 us (4%)
  other arithmetic  6.52 us (2%)
  local copies, waits for them, and re-layouts  3.24 us (1%)
    reduce_scatter x1, waiting for transfers between devices, per_device(): lax.psum_scatter(term_vals, ('sec', 'hid'), scatter_dimension=1, tiled=True)  81.7 us
    all_gather x1, waiting for transfers between devices, per_device(): lax.all_gather(picked_rows, ('sec', 'hid'), axis=1, tiled=True)  71.4 us
    all_gather x1, blocking collectives, per_device(): gathered = lax.all_gather(normed, 'exp', axis=0, tiled=True)  51.2 us
    all_to_all x1, starting transfers between devices, per_device(): lax.all_to_all(outgoing.astype(jnp.bfloat16), 'exp', split_axis=0, concat...  21 us
    psum x1, blocking collectives, per_device(): square_total = lax.psum(one_axis, 'hid')  19.5 us
    all_to_all x1, waiting for transfers between devices, per_device(): lax.all_to_all(outgoing.astype(jnp.bfloat16), 'exp', split_axis=0, concat...  17.2 us
    dot_general x1, matrix products, per_device(): jnp.dot(activated, down_local, preferred_element_type=jnp.float32)  8.64 us
  transfers between devices with their start and end apart: 3, of which 3 were waited for; matrix products, arithmetic and copies ran while one was open for 0% of the time, Pallas kernels for 0%

profile of v1, /device:TPU:9, one launch (start us, length us, event | category | flops | bytes accessed | tf_op | source)
XLA Modules:
  0.0 301.4 jit_solution(3514616078091753310)
XLA Ops:
  6.5 0.8 compare_reduce_fusion
  7.4 0.2 reduce-window.4
  7.6 0.1 select_reduce_fusion.1
  7.7 0.1 fusion.16
  7.9 0.8 fusion.15
  8.7 3.8 %psum.14 = f32[32]{0:T(128)S(1)} all-reduce(f32[32]{0:T(128)S(1)} %fusion.15), channel_id=1, replica_groups=mesh['sec'=2,'exp'=32,'hid'=8] {'sec'}, use_global_device_ids=true, to_apply=%region_5.6 | all-reduce | flops 32 | bytes 256 | tf_op jit(solution)/shard_map/psum | solution.py:33
  12.5 19.5 %psum.15 = f32[32]{0:T(128)S(1)} all-reduce(f32[32]{0:T(128)S(1)} %psum.14), channel_id=1, replica_groups=mesh['sec'=2,'exp'=32,'hid'=8] {'hid'}, use_global_device_ids=true, to_apply=%region_6.7 | all-reduce | flops 32 | bytes 256 | tf_op jit(solution)/shard_map/psum | solution.py:34
  31.9 0.7 convert_element_type.37
  32.6 0.8 fusion.14
  33.4 51.2 %all_gather.6 = bf16[1024,256]{1,0:T(8,128)(2,1)S(1)} all-gather(bf16[32,256]{1,0:T(8,128)(2,1)S(1)} %fusion.14), channel_id=1, replica_groups=mesh['sec'=2,'exp'=32,'hid'=8] {'exp'}, dimensions={0}, use_global_device_ids=true | all-gather | bytes 540672 | tf_op jit(solution)/shard_map/all_gather | solution.py:37
  84.6 0.6 gather_fusion
  85.2 0.1 broadcast_bitcast_fusion
  85.3 0.9 fusion.6
  86.2 0.0 reduce-scatter.2.cloned.1.call-start
  86.3 71.4 %all-gather.2.cloned.1.call-done = bf16[512,4096]{1,0:T(8,128)(2,1)} async-done(((bf16[512,256]{1,0:T(8,128)(2,1)}), bf16[512,4096]{1,0:T(8,128)(2,1)}) %all-gather.2.cloned.1.call-update) | async-done | bytes 4194320 | tf_op jit(solution)/shard_map/all_gather | solution.py:42
  157.6 3.7 %fusion.4 = f32[512,128]{1,0:T(8,128)S(1)} fusion(bf16[512,4096]{1,0:T(8,128)(2,1)} %all-gather.2.cloned.1.call-done, bf16[1,4096,128]{2,1,0:T(8,128)(2,1)} %param.11), kind=kOutput, calls=%fused_computation.8 | convolution fusion | flops 536870912 | bytes 5505024 | tf_op jit(solution)/shard_map/dot_general | solution.py:43
  161.4 8.6 %convolution_convert_fusion = bf16[512,4096]{1,0:T(8,128)(2,1)} fusion(bf16[512,4096]{1,0:T(8,128)(2,1)} %all-gather.2.cloned.1.call-done, bf16[1,128,4096]{2,1,0:T(8,128)(2,1)S(1)} %copy-done, bf16[1,4096,128]{2,1,0:T(8,128)(2,1)S(1)} %copy-done.1, f32[512,128]{1,0:T(8,128)S(1)} %fusion.4), kind=kOutput, calls=%fused_computation.3 | convolution fusion | flops 1076232192 | bytes 10747904 | tf_op jit(solution)/shard_map/dot_general | solution.py:46
  170.0 0.1 broadcast_in_dim.108
  170.1 0.1 broadcast_in_dim.109
  170.2 0.1 broadcast_in_dim.105
  170.3 0.1 broadcast_in_dim.106
  170.4 81.7 %reduce-scatter.2.cloned.1.call-done = bf16[512,256]{1,0:T(8,128)(2,1)} async-done(((bf16[512,4096]{1,0:T(8,128)(2,1)}), bf16[512,256]{1,0:T(8,128)(2,1)}) %reduce-scatter.2.cloned.1.call-update) | async-done | bytes 262160 | tf_op jit(solution)/shard_map/reduce_scatter | solution.py:58
  252.1 1.5 gather_fusion.1
  253.6 1.0 select_convert_fusion
  254.6 21.0 %all-to-all-start = ((bf16[32,32,256]{2,1,0:T(8,128)(2,1)}), bf16[32,32,256]{2,1,0:T(8,128)(2,1)S(1)}, u32[]{:S(2)}, u32[]{:S(2)}) async-start(bf16[32,32,256]{2,1,0:T(8,128)(2,1)} %select_convert_fusion), calls=%async_computation.1 | async-start | bytes 1048576 | tf_op jit(solution)/shard_map/all_to_all | solution.py:67
  275.6 0.1 copy.12
  275.7 0.6 gather_fusion.2
  276.3 0.1 broadcast_select_fusion
  276.4 0.1 copy.13
  276.5 0.1 select_reduce_fusion
  276.6 17.2 %all-to-all-done = bf16[32,32,256]{2,1,0:T(8,128)(2,1)S(1)} async-done(((bf16[32,32,256]{2,1,0:T(8,128)(2,1)}), bf16[32,32,256]{2,1,0:T(8,128)(2,1)S(1)}, u32[]{:S(2)}, u32[]{:S(2)}) %all-to-all-start) | async-done | bytes 524320 | tf_op jit(solution)/shard_map/all_to_all | solution.py:67
  293.8 0.8 multiply_reduce_fusion
  (23 shorter events, 0.1 us)
Async XLA Ops:
  6.5 154.8 %copy-start = (bf16[1,128,4096]{2,1,0:T(8,128)(2,1)S(1)}, bf16[1,128,4096]{2,1,0:T(8,128)(2,1)}, u32[]{:S(2)}) copy-start(bf16[1,128,4096]{2,1,0:T(8,128)(2,1)} %param.13) | copy-start | bytes 3145732
  6.5 154.8 %copy-start.1 = (bf16[1,4096,128]{2,1,0:T(8,128)(2,1)S(1)}, bf16[1,4096,128]{2,1,0:T(8,128)(2,1)}, u32[]{:S(2)}) copy-start(bf16[1,4096,128]{2,1,0:T(8,128)(2,1)} %param.12) | copy-start | bytes 3145732
  6.5 151.1 %all-gather.2.cloned.1.call-start = ((), (), s32[]{:S(2)}) async-start(), calls=%async_computation.2 | async-start | bytes 4456448 | tf_op jit(solution)/shard_map/all_gather | solution.py:42
  86.2 165.9 %reduce-scatter.2.cloned.1.call-start = ((), (), s32[]{:S(2)}) async-start(), calls=%async_computation.3 | async-start | bytes 4456448 | tf_op jit(solution)/shard_map/reduce_scatter | solution.py:58
  170.0 105.6 %copy-start.2 = (s32[8,2]{0,1:T(2,128)S(1)}, s32[8,2]{0,1:T(2,128)}, u32[]{:S(2)}) copy-start(s32[8,2]{0,1:T(2,128)} %param.10) | copy-start | bytes 196
  170.0 106.5 %copy-start.3 = (f32[32,2]{0,1:T(2,128)S(1)}, f32[32,2]{0,1:T(2,128)}, u32[]{:S(2)}) copy-start(f32[32,2]{0,1:T(2,128)} %param.9) | copy-start | bytes 772
  254.6 39.2 %all-to-all-start = ((bf16[32,32,256]{2,1,0:T(8,128)(2,1)}), bf16[32,32,256]{2,1,0:T(8,128)(2,1)S(1)}, u32[]{:S(2)}, u32[]{:S(2)}) async-start(bf16[32,32,256]{2,1,0:T(8,128)(2,1)} %select_convert_fusion), calls=%async_computation.1 | async-start | bytes 1048576 | tf_op jit(solution)/shard_map/all_to_all | solution.py:67
Sparse Core Ops, SparseCore 0:
  86.3 71.2 all-gather.1
  170.2 81.8 reduce-scatter.1
